TPU v7x, 32 devices: a whole 2x2x4 slice. The times are simulated.
32 devices in a mesh: dp: 2 (over x), hst: 4 (over y, core), chip: 4 (over z).
Axes of the slice: x: 2, y: 2, z: 4, core: 2. Of those that a mesh axis runs over, the one named last changes fastest.
Arguments:
- tokens: bfloat16 [512, 8192], P('dp', ('hst', 'chip')), may hold values from -6 to 6
- out_grad: bfloat16 [512, 8192], P('dp', ('hst', 'chip')), may hold values from -6 to 6
- up_blocks: bfloat16 [112, 16, 128, 128], P(('hst', 'chip')), may hold values from -0.125 to 0.125
- up_cols: int32 [112, 16], P(('hst', 'chip')), may hold values from 0 to 63, all different within a row
- down_blocks: bfloat16 [112, 16, 128, 128], P(('hst', 'chip')), may hold values from -0.09375 to 0.09375
- down_cols: int32 [112, 16], P(('hst', 'chip')), may hold values from 0 to 63, all different within a row
Outputs:
- input_grad: bfloat16 [512, 8192], P('dp', ('hst', 'chip'))
- up_grad: float32 [112, 16, 128, 128], P(('hst', 'chip'), None, 'dp')
- down_grad: float32 [112, 16, 128, 128], P(('hst', 'chip'), None, 'dp')
Inputs may be any that keep to these rules, and one draw needn't show every extreme that they name: `up_cols`: each block row names 16 different block columns; every block column is named by some row. `down_cols`: each block row names 16 different block columns; every block column is named by some row.
All inputs are finite; a program needn't handle non-finite values.
Results may differ from a plain program's by a relative error of at most 0.017.
Values may be sent and summed in bfloat16 or wider, within the bound.
A program may use at most 128 MiB of HBM per device.

v0:
```python
import jax
import jax.numpy as jnp
from jax import lax
from jax.sharding import PartitionSpec as P


def local(tokens, out_grad, up_blocks, up_cols, down_blocks, down_cols):
    whole_x, whole_dy = (
        lax.all_gather(tokens, ("hst", "chip"), axis=1, tiled=True),
        lax.all_gather(out_grad, ("hst", "chip"), axis=1, tiled=True),
    )
    tok_rows = whole_x.shape[0]
    block_size = up_blocks.shape[2]
    local_rows = up_blocks.shape[0]
    dblocks = whole_x.shape[1] // block_size
    x_blocks = whole_x.reshape(tok_rows, dblocks, block_size)
    dy_blocks = whole_dy.reshape(tok_rows, dblocks, block_size)
    x_sel = x_blocks[:, up_cols, :]
    dy_sel = dy_blocks[:, down_cols, :]
    pre_act = jnp.einsum("tjkc,jkhc->tjh", x_sel, up_blocks, preferred_element_type=jnp.float32)
    activated = jax.nn.silu(pre_act).astype(jnp.bfloat16)
    down_part = jnp.einsum("tjh,tjkc->jkhc", activated, dy_sel, preferred_element_type=jnp.float32)
    hidden_grad = jnp.einsum(
        "tjkc,jkhc->tjh", dy_sel, down_blocks, preferred_element_type=jnp.float32
    )
    sigmoid_pre = jax.nn.sigmoid(pre_act)
    pre_grad = (hidden_grad * sigmoid_pre * (1.0 + pre_act * (1.0 - sigmoid_pre))).astype(
        jnp.bfloat16
    )
    up_part = jnp.einsum("tjh,tjkc->jkhc", pre_grad, x_sel, preferred_element_type=jnp.float32)
    up_sum, down_sum = (
        lax.psum_scatter(
            up_part.astype(jnp.bfloat16), "dp", scatter_dimension=2, tiled=True
        ).astype(jnp.float32),
        lax.psum_scatter(
            down_part.astype(jnp.bfloat16), "dp", scatter_dimension=2, tiled=True
        ).astype(jnp.float32),
    )
    onehot = (up_cols[:, :, None] == jnp.arange(dblocks, dtype=jnp.int32)[None, None, :]).astype(
        jnp.bfloat16
    )
    dense_up = jnp.einsum(
        "jkb,jkhc->jhbc", onehot, up_blocks, preferred_element_type=jnp.float32
    ).astype(jnp.bfloat16)
    dense_up = dense_up.reshape(local_rows * block_size, dblocks * block_size)
    flat_grad = pre_grad.reshape(tok_rows, local_rows * block_size)
    partial_value = jnp.dot(flat_grad, dense_up, preferred_element_type=jnp.float32)
    summed = lax.psum_scatter(
        partial_value.astype(jnp.bfloat16), ("hst", "chip"), scatter_dimension=1, tiled=True
    )
    return (summed, up_sum, down_sum)


def solution(mesh):
    placed = (
        P("dp", ("hst", "chip")),
        P("dp", ("hst", "chip")),
        P(("hst", "chip"), None, None, None),
        P(("hst", "chip"), None),
        P(("hst", "chip"), None, None, None),
        P(("hst", "chip"), None),
    )
    return jax.shard_map(
        local,
        mesh=mesh,
        in_specs=placed,
        out_specs=(
            P("dp", ("hst", "chip")),
            P(("hst", "chip"), None, "dp", None),
            P(("hst", "chip"), None, "dp", None),
        ),
        check_vma=False,
    )
```

profile of v0, /device:TPU:0, one launch (start us, length us, event | category | flops | bytes accessed | tf_op | source)
XLA Modules:
  0.0 353.3 jit_solution(15198662633239594076)
XLA Ops:
  7.2 0.0 all-gather.5.cloned.1.call-start
  7.2 1.8 copy.44
  9.0 0.0 all-gather.5.cloned.1.call-update
  9.0 0.0 all-gather.3.cloned.1.call-start
  9.1 1.8 copy.40
  10.9 0.0 all-gather.3.cloned.1.call-update
  10.9 0.0 reduce-scatter.6.cloned.1.call-start
  10.9 0.7 compare_select_fusion.1
  11.6 0.1 reshape.25
  11.7 0.7 compare_select_fusion
  12.4 0.1 reshape.33
  12.5 51.4 %all-gather.5.cloned.1.call-done = bf16[256,8192]{0,1:T(8,128)(2,1)} async-done(((bf16[256,512]{0,1:T(8,128)(2,1)}), bf16[256,8192]{0,1:T(8,128)(2,1)}) %all-gather.5.cloned.1.call-update) | async-done | bytes 4194320 | tf_op jit(solution)/shard_map/all_gather | solution.py:9
  63.9 6.4 %copy.45 = bf16[256,64,128]{2,0,1:T(8,128)(2,1)} copy(bf16[256,64,128]{0,2,1:T(8,128)(2,1)} %bitcast.74) | data formatting | bytes 8388608 | tf_op jit(solution)/shard_map/reshape | solution.py:16
  70.2 45.3 %all-gather.3.cloned.1.call-done = bf16[256,8192]{0,1:T(8,128)(2,1)} async-done(((bf16[256,512]{0,1:T(8,128)(2,1)}), bf16[256,8192]{0,1:T(8,128)(2,1)}) %all-gather.3.cloned.1.call-update) | async-done | bytes 4194320 | tf_op jit(solution)/shard_map/all_gather | solution.py:10
  115.6 6.4 %copy.41 = bf16[256,64,128]{2,0,1:T(8,128)(2,1)} copy(bf16[256,64,128]{0,2,1:T(8,128)(2,1)} %bitcast.75) | data formatting | bytes 8388608 | tf_op jit(solution)/shard_map/reshape | solution.py:17
  122.0 8.5 %gather_fusion.1 = bf16[112,256,128]{2,1,0:T(8,128)(2,1)} fusion(bf16[256,64,128]{2,0,1:T(8,128)(2,1)} %copy.45, s32[1024]{0:T(1024)S(1)} %pad_clamp_fusion), kind=kCustom, calls=%fused_computation.1 | custom fusion | bytes 14680512 | tf_op jit(solution)/shard_map/gather | solution.py:18
  130.5 11.3 %copy.46 = bf16[7,16,256,128]{2,3,1,0:T(8,128)(2,1)} copy(bf16[7,16,256,128]{3,2,1,0:T(8,128)(2,1)} %bitcast.67) | data formatting | bytes 14680064 | tf_op jit(solution)/shard_map/gather | solution.py:18
  141.8 8.5 %gather_fusion = bf16[112,256,128]{2,1,0:T(8,128)(2,1)} fusion(bf16[256,64,128]{2,0,1:T(8,128)(2,1)} %copy.41, s32[1024]{0:T(1024)S(1)} %pad_clamp_fusion.1), kind=kCustom, calls=%fused_computation | custom fusion | bytes 14680512 | tf_op jit(solution)/shard_map/gather | solution.py:19
  150.2 0.0 copy-start
  150.2 0.0 copy-start.2
  150.3 0.0 slice-start
  150.3 6.8 %convolution_bitcast_fusion = f32[256,7,128]{0,2,1:T(8,128)S(1)} fusion(bf16[7,16,128,128]{3,2,1,0:T(8,128)(2,1)} %param.8, bf16[256,7,16,128]{3,0,2,1:T(8,128)(2,1)} %bitcast.68), kind=kOutput, calls=%fused_computation.14 | convolution fusion | flops 939524096 | bytes 11927552 | tf_op jit(solution)/shard_map/tjkc,jkhc->tjh/dot_general | solution.py:20
  157.0 0.0 copy-done
  157.0 0.5 copy-done.2
  157.6 0.0 slice-start.1
  157.6 2.5 fusion.17
  160.1 0.0 slice-done
  160.1 0.0 slice-done.1
  160.1 3.9 %convert_bitcast_fusion.1 = bf16[7,16,128,128]{2,3,1,0:T(8,128)(2,1)} fusion(bf16[7,16,256,128]{2,3,1,0:T(8,128)(2,1)S(1)} %bitcast.70, bf16[256,7,128]{0,2,1:T(8,128)(2,1)S(1)} %fusion.17), kind=kOutput, calls=%fused_computation.13 | convolution fusion | flops 941359104 | bytes 11468800 | tf_op jit(solution)/shard_map/tjh,tjkc->jkhc/dot_general | solution.py:30
  164.1 6.5 %copy.50 = bf16[7,16,128,128]{3,1,0,2:T(8,128)(2,1)} copy(bf16[7,16,128,128]{2,3,1,0:T(8,128)(2,1)} %convert_bitcast_fusion.1) | data formatting | bytes 7340032 | tf_op jit(solution)/shard_map/convert_element_type | solution.py:33
  170.5 0.0 reduce-scatter.6.cloned.1.call-update
  170.6 0.2 reduce-scatter.8.cloned.1.call-start
  170.8 11.6 %copy.42 = bf16[7,16,256,128]{2,3,1,0:T(8,128)(2,1)} copy(bf16[7,16,256,128]{3,2,1,0:T(8,128)(2,1)} %bitcast.71) | data formatting | bytes 14680064 | tf_op jit(solution)/shard_map/gather | solution.py:19
  182.3 7.0 %convert_bitcast_fusion = bf16[7,16,128,128]{2,3,1,0:T(8,128)(2,1)} fusion(bf16[7,16,256,128]{2,3,1,0:T(8,128)(2,1)} %copy.42, f32[256,7,128]{0,2,1:T(8,128)S(1)} %convolution_bitcast_fusion), kind=kOutput, calls=%fused_computation.12 | convolution fusion | flops 942505984 | bytes 11927552 | tf_op jit(solution)/shard_map/tjh,tjkc->jkhc/dot_general | solution.py:22
  189.4 0.0 copy-start.1
  189.4 6.6 %copy.52 = bf16[7,16,128,128]{3,1,0,2:T(8,128)(2,1)} copy(bf16[7,16,128,128]{2,3,1,0:T(8,128)(2,1)} %convert_bitcast_fusion) | data formatting | bytes 7340032 | tf_op jit(solution)/shard_map/convert_element_type | solution.py:36
  196.0 0.0 reduce-scatter.8.cloned.1.call-update
  196.0 0.0 reduce-scatter.4.cloned.1.call-start
  196.1 0.0 copy-done.1
  196.1 11.3 %convolution_convert_fusion = bf16[7,64,128,128]{3,1,2,0:T(8,128)(2,1)} fusion(bf16[7,16,128,128]{3,2,1,0:T(8,128)(2,1)} %param.8, s32[7,16]{1,0:T(8,128)S(1)} %copy-done.1), kind=kOutput, calls=%fused_computation.6 | convolution fusion | flops 242228224 | bytes 18350528 | tf_op jit(solution)/shard_map/jkb,jkhc->jhbc/dot_general | solution.py:42
  207.4 17.7 %fusion.3 = bf16[256,8192]{1,0:T(8,128)(2,1)} fusion(bf16[256,896]{0,1:T(8,128)(2,1)S(1)} %bitcast.76, bf16[112,8,64,128]{3,2,1,0:T(8,128)(2,1)} %bitcast.73), kind=kOutput, calls=%fused_computation.5 | convolution fusion | flops 3760193536 | bytes 19333120 | tf_op jit(solution)/shard_map/dot_general | solution.py:47
  225.1 0.0 reduce-scatter.4.cloned.1.call-update
  225.2 0.0 reduce-scatter.6.cloned.1.call-done
  225.2 4.1 %copy.53 = f32[7,16,64,128]{3,2,1,0:T(8,128)} copy(bf16[7,16,64,128]{3,1,0,2:T(8,128)(2,1)} %reduce-scatter.6.cloned.1.call-done) | data formatting | bytes 5505024
  229.3 40.4 %reduce-scatter.8.cloned.1.call-done = bf16[7,16,64,128]{3,1,0,2:T(8,128)(2,1)} async-done(((bf16[7,16,128,128]{3,1,0,2:T(8,128)(2,1)}), bf16[7,16,64,128]{3,1,0,2:T(8,128)(2,1)}) %reduce-scatter.8.cloned.1.call-update) | async-done | bytes 1835024 | tf_op jit(solution)/shard_map/reduce_scatter | solution.py:35
  269.7 3.9 %copy.54 = f32[7,16,64,128]{3,2,1,0:T(8,128)} copy(bf16[7,16,64,128]{3,1,0,2:T(8,128)(2,1)} %reduce-scatter.8.cloned.1.call-done) | data formatting | bytes 5505024
  273.6 73.2 %reduce-scatter.4.cloned.1.call-done = bf16[256,512]{1,0:T(8,128)(2,1)} async-done(((bf16[256,8192]{1,0:T(8,128)(2,1)}), bf16[256,512]{1,0:T(8,128)(2,1)}) %reduce-scatter.4.cloned.1.call-update) | async-done | bytes 262160 | tf_op jit(solution)/shard_map/reduce_scatter | solution.py:48
  (3 shorter events, 0.0 us)
Async XLA Ops:
  7.2 56.7 %all-gather.5.cloned.1.call-start = ((), (), s32[]{:S(2)}) async-start(), calls=%async_computation.4 | async-start | bytes 4456448 | tf_op jit(solution)/shard_map/all_gather | solution.py:9
  9.0 106.6 %all-gather.3.cloned.1.call-start = ((), (), s32[]{:S(2)}) async-start(), calls=%async_computation.3 | async-start | bytes 4456448 | tf_op jit(solution)/shard_map/all_gather | solution.py:10
  10.9 214.3 %reduce-scatter.6.cloned.1.call-start = ((), (), s32[]{:S(2)}) async-start(), calls=%async_computation.6 | async-start | bytes 5505024 | tf_op jit(solution)/shard_map/reduce_scatter | solution.py:32
  150.2 6.8 %copy-start = (bf16[112,256,128]{2,1,0:T(8,128)(2,1)S(1)}, bf16[112,256,128]{2,1,0:T(8,128)(2,1)}, u32[]{:S(2)}) copy-start(bf16[112,256,128]{2,1,0:T(8,128)(2,1)} %gather_fusion) | copy-start | bytes 22020100
  150.2 7.3 %copy-start.2 = (bf16[7,16,128,128]{3,2,1,0:T(8,128)(2,1)S(1)}, bf16[7,16,128,128]{3,2,1,0:T(8,128)(2,1)}, u32[]{:S(2)}) copy-start(bf16[7,16,128,128]{3,2,1,0:T(8,128)(2,1)} %param.10) | copy-start | bytes 11010052
  150.3 9.8 %slice-start = ((s8[7340032]{0:T(1024)(128)(4,1)}), s8[4194304]{0:T(1024)(128)(4,1)S(1)}, s32[]{:S(2)}) async-start(s8[7340032]{0:T(1024)(128)(4,1)} %bitcast.69), calls=%async_computation.8 | async-start | bytes 8388608
  157.6 2.5 slice-start.1
  170.6 99.2 %reduce-scatter.8.cloned.1.call-start = ((), (), s32[]{:S(2)}) async-start(), calls=%async_computation.7 | async-start | bytes 5505024 | tf_op jit(solution)/shard_map/reduce_scatter | solution.py:35
  189.4 6.7 %copy-start.1 = (s32[7,16]{1,0:T(8,128)S(1)}, s32[7,16]{1,0:T(8,128)}, u32[]{:S(2)}) copy-start(s32[7,16]{1,0:T(8,128)} %param.9) | copy-start | bytes 1348
  196.0 150.8 %reduce-scatter.4.cloned.1.call-start = ((), (), s32[]{:S(2)}) async-start(), calls=%async_computation.5 | async-start | bytes 4456448 | tf_op jit(solution)/shard_map/reduce_scatter | solution.py:48
Sparse Core Ops, SparseCore 0:
  10.8 53.0 all-gather.4
  66.7 48.8 all-gather.2
  170.7 47.7 reduce-scatter.5
  220.5 49.1 reduce-scatter.7
  274.0 72.7 reduce-scatter.3
where the time goes:
time: 355 us; the launch traced here: 353 us
  waiting for transfers between devices  210 us (59%)
  local copies, waits for them, and re-layouts  78 us (22%)
  matrix products  49.3 us (14%)
  between operations  13.9 us (4%)
    reduce_scatter x1, waiting for transfers between devices, local(): lax.psum_scatter(partial_value.astype(jnp.bfloat16), ('hst', 'chip'), sca...  73.2 us
    all_gather x1, waiting for transfers between devices, local(): lax.all_gather(tokens, ('hst', 'chip'), axis=1, tiled=True)  51.4 us
    all_gather x1, waiting for transfers between devices, local(): lax.all_gather(out_grad, ('hst', 'chip'), axis=1, tiled=True)  45.3 us
    reduce_scatter x1, waiting for transfers between devices, local(): lax.psum_scatter(down_part.astype(jnp.bfloat16), 'dp', scatter_dimension=...  40.4 us
    gather x2, local copies, waits for them, and re-layouts, local(): dy_sel = dy_blocks[:, down_cols, :]  20 us
    gather x2, local copies, waits for them, and re-layouts, local(): x_sel = x_blocks[:, up_cols, :]  19.8 us
    dot_general x1, matrix products, local(): jnp.dot(flat_grad, dense_up, preferred_element_type=jnp.float32)  17.7 us
    unnamed x14, local copies, waits for them, and re-layouts  12.1 us
  transfers between devices with their start and end apart: 5, of which 4 were waited for; matrix products, arithmetic and copies ran while one was open for 20% of the time, Pallas kernels for 0%

commit v1 on v0

v1 whole, which is shorter than its diff:
```python
import functools

import jax
import jax.numpy as jnp
from jax import lax
from jax.experimental import pallas as pl
from jax.experimental.pallas import tpu as pltpu
from jax.sharding import PartitionSpec as P

NT = (((1,), (1,)), ((), ()))


def rows_kernel(
    split,
    up_cols,
    down_cols,
    me,
    x_ref,
    dy_ref,
    up_ref,
    down_ref,
    in_ref,
    *rest,
):
    outs, (acc, xs, dys, us, ds) = rest[:-5], rest[-5:]
    row = pl.program_id(0)
    width = up_ref.shape[-1]
    per_shard = x_ref.shape[2] // width
    count = up_ref.shape[1]

    @pl.when(row == 0)
    def _():
        acc[...] = jnp.zeros_like(acc)

    def place(col):
        return col // per_shard, pl.ds(pl.multiple_of((col % per_shard) * width, width), width)

    for k in range(count):
        lanes = pl.ds(k * width, width)
        shard, at = place(up_cols[row, k])
        xs[:, lanes] = x_ref[shard, :, at]
        shard, at = place(down_cols[row, k])
        dys[:, lanes] = dy_ref[shard, :, at]
        us[:, lanes] = up_ref[0, k]
        ds[:, lanes] = down_ref[0, k]
    pre = lax.dot_general(us[...], xs[...], NT, preferred_element_type=jnp.float32)
    hid = lax.dot_general(ds[...], dys[...], NT, preferred_element_type=jnp.float32)
    sig = 1.0 / (1.0 + jnp.exp(-pre))
    act = (pre * sig).astype(jnp.bfloat16)
    pre_grad_f = hid * sig * (1.0 + pre * (1.0 - sig))
    pre_grad = pre_grad_f.astype(jnp.bfloat16)
    pre_grad_t = pre_grad_f.T.astype(jnp.bfloat16)

    step = 4
    for base in range(0, count, step):
        lanes = pl.ds(base * width, step * width)
        up_part = jnp.dot(pre_grad, xs[:, lanes], preferred_element_type=jnp.float32)
        down_part = jnp.dot(act, dys[:, lanes], preferred_element_type=jnp.float32)
        back = jnp.dot(pre_grad_t, us[:, lanes], preferred_element_type=jnp.float32)
        for i in range(step):
            k = base + i
            cut = slice(i * width, (i + 1) * width)
            for part, out in ((up_part, outs[: len(outs) // 2]), (down_part, outs[len(outs) // 2 :])):
                block = part[:, cut].astype(jnp.bfloat16)
                if split:
                    half = width // 2
                    first = me[0] == 0
                    out[0][0, k] = jnp.where(first, block[:half], block[half:])
                    out[1][0, k] = jnp.where(first, block[half:], block[:half])
                else:
                    out[0][0, k] = block
            shard, at = place(up_cols[row, k])
            acc[shard, :, at] += back[:, cut]

    @pl.when(row == pl.num_programs(0) - 1)
    def _():
        for s in range(acc.shape[0]):
            in_ref[s] = acc[s].astype(jnp.bfloat16)


def rows_call(split, whole_x, whole_dy, up_blocks, up_cols, down_blocks, down_cols):
    rows, count, width, _ = up_blocks.shape
    shards, tok, part = whole_x.shape
    out_h = width // 2 if split else width
    n_out = 4 if split else 2
    whole = pl.BlockSpec(memory_space=pltpu.VMEM)
    smem = pl.BlockSpec(memory_space=pltpu.SMEM)

    def block(h):
        return pl.BlockSpec((1, count, h, width), lambda r: (r, 0, 0, 0))

    me = lax.axis_index("dp").astype(jnp.int32).reshape(1)
    flops = 10 * tok * rows * count * width * width
    return pl.pallas_call(
        functools.partial(rows_kernel, split),
        grid=(rows,),
        in_specs=[smem, smem, smem, whole, whole, block(width), block(width)],
        out_specs=[whole] + [block(out_h)] * n_out,
        out_shape=[jax.ShapeDtypeStruct(whole_x.shape, jnp.bfloat16)]
        + [jax.ShapeDtypeStruct((rows, count, out_h, width), jnp.bfloat16)] * n_out,
        scratch_shapes=[
            pltpu.VMEM(whole_x.shape, jnp.float32),
            pltpu.VMEM((tok, count * width), jnp.bfloat16),
            pltpu.VMEM((tok, count * width), jnp.bfloat16),
            pltpu.VMEM((width, count * width), jnp.bfloat16),
            pltpu.VMEM((width, count * width), jnp.bfloat16),
        ],
        compiler_params=pltpu.CompilerParams(
            dimension_semantics=("arbitrary",), vmem_limit_bytes=56 * 2**20
        ),
        cost_estimate=pl.CostEstimate(
            flops=flops, bytes_accessed=30 * 2**20, transcendentals=rows * width * tok
        ),
    )(up_cols, down_cols, me, whole_x, whole_dy, up_blocks, down_blocks)


def local(n_dp, tokens, out_grad, up_blocks, up_cols, down_blocks, down_cols):
    whole_x = lax.all_gather(tokens, ("hst", "chip"), axis=0, tiled=False)
    whole_dy = lax.all_gather(out_grad, ("hst", "chip"), axis=0, tiled=False)
    split = n_dp == 2
    partial_value, *grads = rows_call(
        split, whole_x, whole_dy, up_blocks, up_cols, down_blocks, down_cols
    )
    if split:
        swap = [(0, 1), (1, 0)]
        sums = [
            grads[i].astype(jnp.float32)
            + lax.ppermute(grads[i + 1], "dp", swap).astype(jnp.float32)
            for i in (0, 2)
        ]
    else:
        sums = [
            lax.psum_scatter(g, "dp", scatter_dimension=2, tiled=True).astype(jnp.float32)
            for g in grads
        ]
    summed = lax.psum_scatter(
        partial_value, ("hst", "chip"), scatter_dimension=0, tiled=False
    )
    return (summed, *sums)


def solution(mesh):
    placed = (
        P("dp", ("hst", "chip")),
        P("dp", ("hst", "chip")),
        P(("hst", "chip"), None, None, None),
        P(("hst", "chip"), None),
        P(("hst", "chip"), None, None, None),
        P(("hst", "chip"), None),
    )
    return jax.shard_map(
        functools.partial(local, mesh.shape["dp"]),
        mesh=mesh,
        in_specs=placed,
        out_specs=(
            P("dp", ("hst", "chip")),
            P(("hst", "chip"), None, "dp", None),
            P(("hst", "chip"), None, "dp", None),
        ),
        check_vma=False,
    )
```

time: 355 us -> 226 us (0.64)
  local copies, waits for them, and re-layouts: 78 us -> 0.01 us
  matrix products: 49.3 us -> 0 us
  waiting for transfers between devices: 210 us -> 184 us
  Pallas kernels: 0 us -> 20.8 us
  other arithmetic: 1.39 us -> 5.23 us
    reduce_scatter x3 -> x1, waiting for transfers between devices: 114 us -> 0.01 us  [local(): lax.psum_scatter(partial_value, ('hst', 'chip'), scatter_dimension=0, til...]
    ppermute x0 -> x2, waiting for transfers between devices: none -> 77 us  [local(): lax.ppermute(grads[i + 1], 'dp', swap).astype(jnp.float32)]
    dot_general x6 -> x0, matrix products: 49.3 us -> none  [the longest x1 17.7 us: local(): jnp.dot(flat_grad, dense_up, preferred_element_type=jnp.float32)]
    gather x4 -> x0, local copies, waits for them, and re-layouts: 39.8 us -> none  [the longest x2 20 us: local(): dy_sel = dy_blocks[:, down_cols, :]]
    pallas_call x0 -> x1, Pallas kernels: none -> 20.8 us  [rows_call(): pl.pallas_call(functools.partial(rows_kernel, split), grid=(rows,), in_sp...]
    convert_element_type x2 -> x0, local copies, waits for them, and re-layouts: 13.1 us -> none  [the longest x1 6.64 us: local(): down_part.astype(jnp.bfloat16)]
    reshape x2 -> x0, local copies, waits for them, and re-layouts: 12.8 us -> none  [the longest x1 6.41 us: local(): dy_blocks = whole_dy.reshape(tok_rows, dblocks, block_size)]
    unnamed x14 -> x4, local copies, waits for them, and re-layouts: 12.1 us -> 0.01 us
  transfers between devices with their start and end apart: 5 -> 5, of which waited for: 4 -> 4; matrix products, arithmetic and copies ran while one was open for 20% -> 2% of each run, Pallas kernels for 0% -> 0%
where the time goes in v1:
time: 226 us
  waiting for transfers between devices  184 us (81%)
  Pallas kernels  20.8 us (9%)
  between operations  13.8 us (6%)
  other arithmetic  5.23 us (2%)
    ppermute x2, waiting for transfers between devices, local(): lax.ppermute(grads[i + 1], 'dp', swap).astype(jnp.float32)  77 us
    all_gather x1, waiting for transfers between devices, local(): whole_x = lax.all_gather(tokens, ('hst', 'chip'), axis=0, tiled=False)  54.6 us
    all_gather x1, waiting for transfers between devices, local(): whole_dy = lax.all_gather(out_grad, ('hst', 'chip'), axis=0, tiled=False)  51.1 us
    pallas_call x1, Pallas kernels, rows_call(): pl.pallas_call(functools.partial(rows_kernel, split), grid=(rows,), in_sp...  20.8 us
    add x2, other arithmetic, local(): grads[i].astype(jnp.float32)  5.23 us
  transfers between devices with their start and end apart: 5, of which 4 were waited for; matrix products, arithmetic and copies ran while one was open for 2% of the time, Pallas kernels for 0%

profile of v1, /device:TPU:0, one launch (start us, length us, event | category | flops | bytes accessed | tf_op | source)
XLA Modules:
  0.0 226.1 jit_solution(11024831387850065969)
XLA Ops:
  7.2 0.0 all-gather.5.cloned.1.call-start
  7.2 0.7 all-gather.5.cloned.1.call-update
  7.9 0.0 all-gather.7.cloned.1.call-start
  7.9 0.7 all-gather.7.cloned.1.call-update
  8.6 0.0 reduce-scatter.2.cloned.1.call-start
  8.7 54.6 %all-gather.5.cloned.1.call-done = bf16[4096,512]{1,0:T(8,128)(2,1)} async-done(((bf16[256,512]{1,0:T(8,128)(2,1)}), bf16[4096,512]{1,0:T(8,128)(2,1)}) %all-gather.5.cloned.1.call-update) | async-done | bytes 4194320 | tf_op jit(solution)/shard_map/all_gather | solution.py:118
  63.3 51.1 %all-gather.7.cloned.1.call-done = bf16[4096,512]{1,0:T(8,128)(2,1)} async-done(((bf16[256,512]{1,0:T(8,128)(2,1)}), bf16[4096,512]{1,0:T(8,128)(2,1)}) %all-gather.7.cloned.1.call-update) | async-done | bytes 4194320 | tf_op jit(solution)/shard_map/all_gather | solution.py:119
  114.4 20.8 %shard_map.85 = (bf16[16,256,512]{2,1,0:T(8,128)(2,1)}, bf16[7,16,64,128]{3,2,1,0:T(8,128)(2,1)}, bf16[7,16,64,128]{3,2,1,0:T(8,128)(2,1)}, bf16[7,16,64,128]{3,2,1,0:T(8,128)(2,1)}, bf16[7,16,64,128]{3,2,1,0:T(8,128)(2,1)}) custom-call(s32[7,16]{1,0:T(8,128)} %up_cols.1, s32[7,16]{1,0:T(8,128)} %down_cols.1, s32[1]{0:T(128)} %bitcast.me, ...), custom_call_target="tpu_custom_call" | custom-call | flops 4697620480 | bytes 31457280 | tf_op jit(solution)/shard_map/pallas_call | solution.py:94
  135.2 0.0 copy-start.1
  135.2 0.0 reduce-scatter.2.cloned.1.call-update
  135.2 1.5 collective-permute-start
  136.8 0.6 collective-permute-start.1
  137.3 41.1 %collective-permute-done = bf16[7,16,64,128]{3,2,1,0:T(8,128)(2,1)S(1)} collective-permute-done((bf16[7,16,64,128]{3,2,1,0:T(8,128)(2,1)}, bf16[7,16,64,128]{3,2,1,0:T(8,128)(2,1)S(1)}, u32[]{:S(2)}, u32[]{:S(2)}) %collective-permute-start) | collective-permute-done | bytes 1835040 | tf_op jit(solution)/shard_map/ppermute | solution.py:128
  178.4 0.0 copy-done.1
  178.4 0.0 copy-start
  178.4 2.6 %convert_add_fusion.1 = f32[7,16,64,128]{3,2,1,0:T(8,128)} fusion(bf16[7,16,64,128]{3,2,1,0:T(8,128)(2,1)S(1)} %collective-permute-done, bf16[7,16,64,128]{3,2,1,0:T(8,128)(2,1)S(1)} %copy-done.1), kind=kLoop, calls=%fused_computation.1 | loop fusion | flops 2752512 | bytes 7340032 | tf_op jit(solution)/shard_map/add | solution.py:127
  181.0 36.0 %collective-permute-done.1 = bf16[7,16,64,128]{3,2,1,0:T(8,128)(2,1)S(1)} collective-permute-done((bf16[7,16,64,128]{3,2,1,0:T(8,128)(2,1)}, bf16[7,16,64,128]{3,2,1,0:T(8,128)(2,1)S(1)}, u32[]{:S(2)}, u32[]{:S(2)}) %collective-permute-start.1) | collective-permute-done | bytes 1835040 | tf_op jit(solution)/shard_map/ppermute | solution.py:128
  217.0 0.0 copy-done
  217.0 2.6 %convert_add_fusion = f32[7,16,64,128]{3,2,1,0:T(8,128)} fusion(bf16[7,16,64,128]{3,2,1,0:T(8,128)(2,1)S(1)} %collective-permute-done.1, bf16[7,16,64,128]{3,2,1,0:T(8,128)(2,1)S(1)} %copy-done), kind=kLoop, calls=%fused_computation | loop fusion | flops 2752512 | bytes 7340032 | tf_op jit(solution)/shard_map/add | solution.py:127
  219.6 0.0 reduce-scatter.2.cloned.1.call-done
Async XLA Ops:
  7.2 56.1 %all-gather.5.cloned.1.call-start = ((), (), s32[]{:S(2)}) async-start(), calls=%async_computation.2 | async-start | bytes 4456448 | tf_op jit(solution)/shard_map/all_gather | solution.py:118
  7.9 106.5 %all-gather.7.cloned.1.call-start = ((), (), s32[]{:S(2)}) async-start(), calls=%async_computation.3 | async-start | bytes 4456448 | tf_op jit(solution)/shard_map/all_gather | solution.py:119
  8.6 211.0 %reduce-scatter.2.cloned.1.call-start = ((), (), s32[]{:S(2)}) async-start(), calls=%async_computation.1 | async-start | bytes 4456448 | tf_op jit(solution)/shard_map/reduce_scatter | solution.py:136
  135.2 43.2 %copy-start.1 = (bf16[7,16,64,128]{3,2,1,0:T(8,128)(2,1)S(1)}, bf16[7,16,64,128]{3,2,1,0:T(8,128)(2,1)}, u32[]{:S(2)}) copy-start(bf16[7,16,64,128]{3,2,1,0:T(8,128)(2,1)} %get-tuple-element.9) | copy-start | bytes 5505028
  135.2 43.2 %collective-permute-start = (bf16[7,16,64,128]{3,2,1,0:T(8,128)(2,1)}, bf16[7,16,64,128]{3,2,1,0:T(8,128)(2,1)S(1)}, u32[]{:S(2)}, u32[]{:S(2)}) collective-permute-start(bf16[7,16,64,128]{3,2,1,0:T(8,128)(2,1)} %get-tuple-element.10), channel_id=1, source_target_pairs={{0,16},{16,0},{1,17},{17,1},{2,18},{18,2},{3,19},{19,3},{4,20},{20... | collective-permute-start | bytes 5505032 | tf_op jit(solution)/shard_map/ppermute | solution.py:128
  136.8 80.2 %collective-permute-start.1 = (bf16[7,16,64,128]{3,2,1,0:T(8,128)(2,1)}, bf16[7,16,64,128]{3,2,1,0:T(8,128)(2,1)S(1)}, u32[]{:S(2)}, u32[]{:S(2)}) collective-permute-start(bf16[7,16,64,128]{3,2,1,0:T(8,128)(2,1)} %get-tuple-element.12), channel_id=1, source_target_pairs={{0,16},{16,0},{1,17},{17,1},{2,18},{18,2},{3,19},{19,3},{4,20},{20... | collective-permute-start | bytes 5505032 | tf_op jit(solution)/shard_map/ppermute | solution.py:128
  178.4 38.6 %copy-start = (bf16[7,16,64,128]{3,2,1,0:T(8,128)(2,1)S(1)}, bf16[7,16,64,128]{3,2,1,0:T(8,128)(2,1)}, u32[]{:S(2)}) copy-start(bf16[7,16,64,128]{3,2,1,0:T(8,128)(2,1)} %get-tuple-element.11) | copy-start | bytes 5505028
Sparse Core Ops, SparseCore 0:
  10.2 53.0 all-gather.4
  65.5 48.8 all-gather.6
  135.4 71.3 reduce-scatter.1

commit v2 on v1

--- a/solution.py
+++ b/solution.py
@@ -114,9 +114,134 @@
     )(up_cols, down_cols, me, whole_x, whole_dy, up_blocks, down_blocks)
 
 
-def local(n_dp, tokens, out_grad, up_blocks, up_cols, down_blocks, down_cols):
-    whole_x = lax.all_gather(tokens, ("hst", "chip"), axis=0, tiled=False)
-    whole_dy = lax.all_gather(out_grad, ("hst", "chip"), axis=0, tiled=False)
+MESH = pl.DeviceIdType.MESH
+ALONG_UP, ALONG_DOWN, ACROSS, SIDE = range(4)
+
+
+def gather_kernel(n_chip, x_ref, dy_ref, x_out, dy_out, send_sem, recv_sem, own_sem):
+    hst, z = lax.axis_index("hst"), lax.axis_index("chip")
+    far, c = hst // 2, hst % 2
+    own = hst * n_chip + z
+    ins, outs = (x_ref, dy_ref), (x_out, dy_out)
+    not_last, not_first = z < n_chip - 1, z > 0
+    peers = {
+        ALONG_UP: {"hst": hst, "chip": (z + 1) % n_chip},
+        ALONG_DOWN: {"hst": hst, "chip": (z + n_chip - 1) % n_chip},
+        ACROSS: {"hst": (1 - far) * 2 + c, "chip": z},
+        SIDE: {"hst": far * 2 + 1 - c, "chip": z},
+    }
+
+    barrier = pltpu.get_barrier_semaphore()
+
+    def greet(way):
+        pl.semaphore_signal(barrier, inc=1, device_id=peers[way], device_id_type=MESH)
+
+    greet(ACROSS)
+    greet(SIDE)
+    pl.when(not_last)(lambda: greet(ALONG_UP))
+    pl.when(not_first)(lambda: greet(ALONG_DOWN))
+    inner = jnp.logical_and(not_last, not_first)
+    pl.when(inner)(lambda: pl.semaphore_wait(barrier, 4))
+    pl.when(jnp.logical_not(inner))(lambda: pl.semaphore_wait(barrier, 3))
+
+    def copy(a, way, shard, source=None):
+        return pltpu.make_async_remote_copy(
+            src_ref=outs[a].at[shard] if source is None else source,
+            dst_ref=outs[a].at[shard],
+            send_sem=send_sem.at[a, way, shard],
+            recv_sem=recv_sem.at[a, shard],
+            device_id=peers[way],
+            device_id_type=MESH,
+        )
+
+    def each(act):
+        for t in range(n_chip + 1):
+            for a in range(2):
+                if t == 0:
+                    act(a, (), own, None, True)
+                elif t < n_chip:
+                    below = z - t
+                    act(a, (ALONG_UP,), hst * n_chip + below, below >= 0, False)
+                    above = z + t
+                    act(a, (ALONG_DOWN,), hst * n_chip + above, above < n_chip, False)
+            for a in range(2):
+                if t >= 1:
+                    base = ((1 - far) * 2 + c) * n_chip
+                    if t == 1:
+                        act(a, None, base + z, None, False)
+                    else:
+                        act(a, None, base + z - (t - 1), z - (t - 1) >= 0, False)
+                        act(a, None, base + z + (t - 1), z + (t - 1) < n_chip, False)
+
+    def guarded(condition, run):
+        if condition is None:
+            run()
+        else:
+            pl.when(condition)(run)
+
+    def forward(a, ways, shard, condition, is_own):
+        def run():
+            if not is_own:
+                copy(a, SIDE, shard).wait_recv()
+            source = ins[a] if is_own else None
+            if ways is not None:
+                if is_own or ALONG_UP in ways:
+                    pl.when(not_last)(lambda: copy(a, ALONG_UP, shard, source).start())
+                if is_own or ALONG_DOWN in ways:
+                    pl.when(not_first)(lambda: copy(a, ALONG_DOWN, shard, source).start())
+                copy(a, ACROSS, shard, source).start()
+            copy(a, SIDE, shard, source).start()
+
+        guarded(condition, run)
+
+    def finish(a, ways, shard, condition, is_own):
+        def run():
+            source = ins[a] if is_own else None
+            if ways is not None:
+                if is_own or ALONG_UP in ways:
+                    pl.when(not_last)(lambda: copy(a, ALONG_UP, shard, source).wait_send())
+                if is_own or ALONG_DOWN in ways:
+                    pl.when(not_first)(lambda: copy(a, ALONG_DOWN, shard, source).wait_send())
+                copy(a, ACROSS, shard, source).wait_send()
+            copy(a, SIDE, shard, source).wait_send()
+
+        guarded(condition, run)
+
+    each(forward)
+    mine = [pltpu.make_async_copy(ins[a], outs[a].at[own], own_sem.at[a]) for a in range(2)]
+    for m in mine:
+        m.start()
+    for half in range(2):
+        for place in range(n_chip):
+            for a in range(2):
+                copy(a, SIDE, (half * 2 + 1 - c) * n_chip + place).wait_recv()
+    each(finish)
+    for m in mine:
+        m.wait()
+
+
+def gather_call(n_hst, n_chip, tokens, out_grad):
+    if n_hst != 4:
+        return [
+            lax.all_gather(v, ("hst", "chip"), axis=0, tiled=False) for v in (tokens, out_grad)
+        ]
+    shards = n_hst * n_chip
+    return pl.pallas_call(
+        functools.partial(gather_kernel, n_chip),
+        in_specs=[pl.BlockSpec(memory_space=pltpu.VMEM)] * 2,
+        out_specs=[pl.BlockSpec(memory_space=pl.ANY)] * 2,
+        out_shape=[jax.ShapeDtypeStruct((shards, *v.shape), v.dtype) for v in (tokens, out_grad)],
+        scratch_shapes=[
+            pltpu.SemaphoreType.DMA((2, 4, shards)),
+            pltpu.SemaphoreType.DMA((2, shards)),
+            pltpu.SemaphoreType.DMA((2,)),
+        ],
+        compiler_params=pltpu.CompilerParams(collective_id=0, has_side_effects=True),
+    )(tokens, out_grad)
+
+
+def local(n_dp, n_hst, n_chip, tokens, out_grad, up_blocks, up_cols, down_blocks, down_cols):
+    whole_x, whole_dy = gather_call(n_hst, n_chip, tokens, out_grad)
     split = n_dp == 2
     partial_value, *grads = rows_call(
         split, whole_x, whole_dy, up_blocks, up_cols, down_blocks, down_cols
@@ -149,7 +274,7 @@
         P(("hst", "chip"), None),
     )
     return jax.shard_map(
-        functools.partial(local, mesh.shape["dp"]),
+        functools.partial(local, mesh.shape["dp"], mesh.shape["hst"], mesh.shape["chip"]),
         mesh=mesh,
         in_specs=placed,
         out_specs=(

time: 226 us -> 174 us (0.77)
  waiting for transfers between devices: 184 us -> 77.3 us
  Pallas kernels: 20.8 us -> 74.8 us
    all_gather x2 -> x0, waiting for transfers between devices: 106 us -> none  [the longest x1 54.6 us: local(): whole_x = lax.all_gather(tokens, ('hst', 'chip'), axis=0, tiled=False)]
    pallas_call x0 -> x1, Pallas kernels: none -> 54 us  [gather_call(): pl.pallas_call(functools.partial(gather_kernel, n_chip), in_specs=[pl.Blo...]
  transfers between devices with their start and end apart: 5 -> 3, of which waited for: 4 -> 2; matrix products, arithmetic and copies ran while one was open for 2% -> 3% of each run, Pallas kernels for 0% -> 0%
where the time goes in v2:
time: 174 us
  waiting for transfers between devices  77.3 us (44%)
  Pallas kernels  74.8 us (43%)
  between operations  14 us (8%)
  other arithmetic  5.23 us (3%)
  starting transfers between devices  2.13 us (1%)
    ppermute x2, waiting for transfers between devices, local(): lax.ppermute(grads[i + 1], 'dp', swap).astype(jnp.float32)  77.3 us
    pallas_call x1, Pallas kernels, gather_call(): pl.pallas_call(functools.partial(gather_kernel, n_chip), in_specs=[pl.Blo...  54 us
    pallas_call x1, Pallas kernels, rows_call(): pl.pallas_call(functools.partial(rows_kernel, split), grid=(rows,), in_sp...  20.8 us
    add x2, other arithmetic, local(): grads[i].astype(jnp.float32)  5.23 us
  transfers between devices with their start and end apart: 3, of which 2 were waited for; matrix products, arithmetic and copies ran while one was open for 3% of the time, Pallas kernels for 0%

profile of v2, /device:TPU:0, one launch (start us, length us, event | category | flops | bytes accessed | tf_op | source)
XLA Modules:
  0.0 173.5 jit_solution(8327308186438907371)
XLA Ops:
  7.2 0.0 reduce-scatter.2.cloned.1.call-start
  7.2 54.0 %shard_map.85 = (bf16[16,256,512]{2,1,0:T(8,128)(2,1)}, bf16[16,256,512]{2,1,0:T(8,128)(2,1)}) custom-call(bf16[256,512]{1,0:T(8,128)(2,1)} %x_ref.1, bf16[256,512]{1,0:T(8,128)(2,1)} %dy_ref.1), custom_call_target="tpu_custom_call" | custom-call | tf_op jit(solution)/shard_map/pallas_call | solution.py:229
  61.2 20.8 %shard_map.86 = (bf16[16,256,512]{2,1,0:T(8,128)(2,1)}, bf16[7,16,64,128]{3,2,1,0:T(8,128)(2,1)}, bf16[7,16,64,128]{3,2,1,0:T(8,128)(2,1)}, bf16[7,16,64,128]{3,2,1,0:T(8,128)(2,1)}, bf16[7,16,64,128]{3,2,1,0:T(8,128)(2,1)}) custom-call(s32[7,16]{1,0:T(8,128)} %up_cols.1, s32[7,16]{1,0:T(8,128)} %down_cols.1, s32[1]{0:T(128)} %bitcast.me, ...), custom_call_target="tpu_custom_call" | custom-call | flops 4697620480 | bytes 31457280 | tf_op jit(solution)/shard_map/pallas_call | solution.py:94
  82.0 0.0 copy-start.1
  82.1 0.0 reduce-scatter.2.cloned.1.call-update
  82.1 1.6 collective-permute-start
  83.6 0.5 collective-permute-start.1
  84.2 41.1 %collective-permute-done = bf16[7,16,64,128]{3,2,1,0:T(8,128)(2,1)S(1)} collective-permute-done((bf16[7,16,64,128]{3,2,1,0:T(8,128)(2,1)}, bf16[7,16,64,128]{3,2,1,0:T(8,128)(2,1)S(1)}, u32[]{:S(2)}, u32[]{:S(2)}) %collective-permute-start) | collective-permute-done | bytes 1835040 | tf_op jit(solution)/shard_map/ppermute | solution.py:253
  125.2 0.0 copy-done.1
  125.2 0.0 copy-start
  125.2 2.6 %convert_add_fusion.1 = f32[7,16,64,128]{3,2,1,0:T(8,128)} fusion(bf16[7,16,64,128]{3,2,1,0:T(8,128)(2,1)S(1)} %collective-permute-done, bf16[7,16,64,128]{3,2,1,0:T(8,128)(2,1)S(1)} %copy-done.1), kind=kLoop, calls=%fused_computation.1 | loop fusion | flops 2752512 | bytes 7340032 | tf_op jit(solution)/shard_map/add | solution.py:252
  127.8 36.2 %collective-permute-done.1 = bf16[7,16,64,128]{3,2,1,0:T(8,128)(2,1)S(1)} collective-permute-done((bf16[7,16,64,128]{3,2,1,0:T(8,128)(2,1)}, bf16[7,16,64,128]{3,2,1,0:T(8,128)(2,1)S(1)}, u32[]{:S(2)}, u32[]{:S(2)}) %collective-permute-start.1) | collective-permute-done | bytes 1835040 | tf_op jit(solution)/shard_map/ppermute | solution.py:253
  164.0 0.0 copy-done
  164.0 2.6 %convert_add_fusion = f32[7,16,64,128]{3,2,1,0:T(8,128)} fusion(bf16[7,16,64,128]{3,2,1,0:T(8,128)(2,1)S(1)} %collective-permute-done.1, bf16[7,16,64,128]{3,2,1,0:T(8,128)(2,1)S(1)} %copy-done), kind=kLoop, calls=%fused_computation | loop fusion | flops 2752512 | bytes 7340032 | tf_op jit(solution)/shard_map/add | solution.py:252
  166.7 0.0 reduce-scatter.2.cloned.1.call-done
Async XLA Ops:
  7.2 159.5 %reduce-scatter.2.cloned.1.call-start = ((), (), s32[]{:S(2)}) async-start(), calls=%async_computation.1 | async-start | bytes 4456448 | tf_op jit(solution)/shard_map/reduce_scatter | solution.py:261
  82.0 43.2 %copy-start.1 = (bf16[7,16,64,128]{3,2,1,0:T(8,128)(2,1)S(1)}, bf16[7,16,64,128]{3,2,1,0:T(8,128)(2,1)}, u32[]{:S(2)}) copy-start(bf16[7,16,64,128]{3,2,1,0:T(8,128)(2,1)} %get-tuple-element.13) | copy-start | bytes 5505028
  82.1 43.2 %collective-permute-start = (bf16[7,16,64,128]{3,2,1,0:T(8,128)(2,1)}, bf16[7,16,64,128]{3,2,1,0:T(8,128)(2,1)S(1)}, u32[]{:S(2)}, u32[]{:S(2)}) collective-permute-start(bf16[7,16,64,128]{3,2,1,0:T(8,128)(2,1)} %get-tuple-element.14), channel_id=1, source_target_pairs={{0,16},{16,0},{1,17},{17,1},{2,18},{18,2},{3,19},{19,3},{4,20},{20... | collective-permute-start | bytes 5505032 | tf_op jit(solution)/shard_map/ppermute | solution.py:253
  83.6 80.4 %collective-permute-start.1 = (bf16[7,16,64,128]{3,2,1,0:T(8,128)(2,1)}, bf16[7,16,64,128]{3,2,1,0:T(8,128)(2,1)S(1)}, u32[]{:S(2)}, u32[]{:S(2)}) collective-permute-start(bf16[7,16,64,128]{3,2,1,0:T(8,128)(2,1)} %get-tuple-element.16), channel_id=1, source_target_pairs={{0,16},{16,0},{1,17},{17,1},{2,18},{18,2},{3,19},{19,3},{4,20},{20... | collective-permute-start | bytes 5505032 | tf_op jit(solution)/shard_map/ppermute | solution.py:253
  125.2 38.8 %copy-start = (bf16[7,16,64,128]{3,2,1,0:T(8,128)(2,1)S(1)}, bf16[7,16,64,128]{3,2,1,0:T(8,128)(2,1)}, u32[]{:S(2)}) copy-start(bf16[7,16,64,128]{3,2,1,0:T(8,128)(2,1)} %get-tuple-element.15) | copy-start | bytes 5505028
Sparse Core Ops, SparseCore 0:
  82.2 72.9 reduce-scatter.1

commit v3 on v2

--- a/solution.py
+++ b/solution.py
@@ -240,6 +240,180 @@
     )(tokens, out_grad)
 
 
+def scatter_kernel(n_chip, part, out, side, cross, up, down, cross_out, line_out, send_sem, recv_sem):
+    hst, z = lax.axis_index("hst"), lax.axis_index("chip")
+    far, c = hst // 2, hst % 2
+    not_last, not_first = z < n_chip - 1, z > 0
+    peers = {
+        ALONG_UP: {"hst": hst, "chip": (z + 1) % n_chip},
+        ALONG_DOWN: {"hst": hst, "chip": (z + n_chip - 1) % n_chip},
+        ACROSS: {"hst": (1 - far) * 2 + c, "chip": z},
+        SIDE: {"hst": far * 2 + 1 - c, "chip": z},
+    }
+    barrier = pltpu.get_barrier_semaphore()
+
+    def greet(way):
+        pl.semaphore_signal(barrier, inc=1, device_id=peers[way], device_id_type=MESH)
+
+    greet(ACROSS)
+    greet(SIDE)
+    pl.when(not_last)(lambda: greet(ALONG_UP))
+    pl.when(not_first)(lambda: greet(ALONG_DOWN))
+    inner = jnp.logical_and(not_last, not_first)
+    pl.when(inner)(lambda: pl.semaphore_wait(barrier, 4))
+    pl.when(jnp.logical_not(inner))(lambda: pl.semaphore_wait(barrier, 3))
+
+    def copy(way, source, target, slot):
+        return pltpu.make_async_remote_copy(
+            src_ref=source,
+            dst_ref=target,
+            send_sem=send_sem.at[way, slot],
+            recv_sem=recv_sem.at[way, slot],
+            device_id=peers[way],
+            device_id_type=MESH,
+        )
+
+    def side_copy(half, place):
+        slot = half * n_chip + place
+        return copy(SIDE, part.at[(half * 2 + 1 - c) * n_chip + place], side.at[slot], slot)
+
+    def cross_copy(place):
+        return copy(ACROSS, cross_out.at[place], cross.at[place], place)
+
+    def up_copy(place):
+        return copy(ALONG_UP, line_out.at[place], up.at[place], place)
+
+    def down_copy(place):
+        return copy(ALONG_DOWN, line_out.at[place], down.at[place], place)
+
+    def each(act):
+        for t in range(n_chip - 1, 0, -1):
+            pl.when(z + t < n_chip)(lambda t=t: act(z + t, 1))
+            pl.when(z - t >= 0)(lambda t=t: act(z - t, -1))
+        act(z, 0)
+
+    rows = part.shape[1]
+    chunk = 32 if rows % 32 == 0 else rows
+
+    def total(store, terms):
+        def body(i, carry):
+            at = pl.ds(pl.multiple_of(i * chunk, chunk), chunk)
+            value = None
+            for ref, slot in terms:
+                term = ref[slot, at, :].astype(jnp.float32)
+                value = term if value is None else value + term
+            store(at, value.astype(jnp.bfloat16))
+            return carry
+
+        lax.fori_loop(0, rows // chunk, body, 0)
+
+    def to(ref, slot):
+        def store(at, value):
+            ref[slot, at, :] = value
+
+        return store
+
+    def to_out(at, value):
+        out[at, :] = value
+
+    each(lambda place, _: side_copy(1 - far, place).start())
+    each(lambda place, _: side_copy(far, place).start())
+
+    def cross_step(place, _):
+        slot = (1 - far) * n_chip + place
+        side_copy(1 - far, place).wait_recv()
+        total(to(cross_out, place), [(part, ((1 - far) * 2 + c) * n_chip + place), (side, slot)])
+        cross_copy(place).start()
+
+    each(cross_step)
+
+    def line_step(place, sign):
+        slot = far * n_chip + place
+        side_copy(far, place).wait_recv()
+        cross_copy(place).wait_recv()
+        base = [(part, (far * 2 + c) * n_chip + place), (side, slot), (cross, place)]
+        if sign > 0:
+
+            @pl.when(not_first)
+            def _():
+                up_copy(place).wait_recv()
+                total(to(line_out, place), base + [(up, place)])
+
+            @pl.when(jnp.logical_not(not_first))
+            def _():
+                total(to(line_out, place), base)
+
+            up_copy(place).start()
+        elif sign < 0:
+
+            @pl.when(not_last)
+            def _():
+                down_copy(place).wait_recv()
+                total(to(line_out, place), base + [(down, place)])
+
+            @pl.when(jnp.logical_not(not_last))
+            def _():
+                total(to(line_out, place), base)
+
+            down_copy(place).start()
+        else:
+
+            @pl.when(inner)
+            def _():
+                up_copy(place).wait_recv()
+                down_copy(place).wait_recv()
+                total(to_out, base + [(up, place), (down, place)])
+
+            @pl.when(jnp.logical_not(not_first))
+            def _():
+                down_copy(place).wait_recv()
+                total(to_out, base + [(down, place)])
+
+            @pl.when(jnp.logical_not(not_last))
+            def _():
+                up_copy(place).wait_recv()
+                total(to_out, base + [(up, place)])
+
+    each(line_step)
+
+    def finish(place, sign):
+        side_copy(1 - far, place).wait_send()
+        side_copy(far, place).wait_send()
+        cross_copy(place).wait_send()
+        if sign > 0:
+            up_copy(place).wait_send()
+        elif sign < 0:
+            down_copy(place).wait_send()
+
+    each(finish)
+
+
+def scatter_call(n_hst, n_chip, part):
+    if n_hst != 4 or n_chip < 2:
+        return lax.psum_scatter(part, ("hst", "chip"), scatter_dimension=0, tiled=False)
+    shards, rows, width = part.shape
+    whole = pl.BlockSpec(memory_space=pltpu.VMEM)
+
+    def slots(count):
+        return pltpu.VMEM((count, rows, width), jnp.bfloat16)
+
+    return pl.pallas_call(
+        functools.partial(scatter_kernel, n_chip),
+        in_specs=[whole],
+        out_specs=whole,
+        out_shape=jax.ShapeDtypeStruct((rows, width), jnp.bfloat16),
+        scratch_shapes=[slots(2 * n_chip)]
+        + [slots(n_chip)] * 5
+        + [pltpu.SemaphoreType.DMA((4, 2 * n_chip))] * 2,
+        compiler_params=pltpu.CompilerParams(
+            collective_id=1, has_side_effects=True, vmem_limit_bytes=24 * 2**20
+        ),
+        cost_estimate=pl.CostEstimate(
+            flops=shards * rows * width, bytes_accessed=120 * 2**20, transcendentals=0
+        ),
+    )(part)
+
+
 def local(n_dp, n_hst, n_chip, tokens, out_grad, up_blocks, up_cols, down_blocks, down_cols):
     whole_x, whole_dy = gather_call(n_hst, n_chip, tokens, out_grad)
     split = n_dp == 2
@@ -258,9 +432,7 @@
             lax.psum_scatter(g, "dp", scatter_dimension=2, tiled=True).astype(jnp.float32)
             for g in grads
         ]
-    summed = lax.psum_scatter(
-        partial_value, ("hst", "chip"), scatter_dimension=0, tiled=False
-    )
+    summed = scatter_call(n_hst, n_chip, partial_value)
     return (summed, *sums)
 
 

time: 174 us -> 161 us (0.925)
  waiting for transfers between devices: 77.3 us -> 40.7 us
  Pallas kernels: 74.8 us -> 109 us
  between operations: 14 us -> 0.66 us
  local copies, waits for them, and re-layouts: 0.01 us -> 2.9 us
    ppermute x2, waiting for transfers between devices: 77.3 us -> 40.7 us  [local(): lax.ppermute(grads[i + 1], 'dp', swap).astype(jnp.float32)]
    pallas_call x0 -> x1, Pallas kernels: none -> 34.4 us  [scatter_call(): pl.pallas_call(functools.partial(scatter_kernel, n_chip), in_specs=[whole...]
    unnamed x4 -> x7, local copies, waits for them, and re-layouts: 0.01 us -> 2.9 us
  transfers between devices with their start and end apart: 3 -> 2, of which waited for: 2 -> 2; matrix products, arithmetic and copies ran while one was open for 3% -> 2% of each run, Pallas kernels for 0% -> 21%
where the time goes in v3:
time: 161 us
  Pallas kernels  109 us (68%)
  waiting for transfers between devices  40.7 us (25%)
  other arithmetic  5.22 us (3%)
  local copies, waits for them, and re-layouts  2.9 us (2%)
  starting transfers between devices  2.06 us (1%)
    pallas_call x1, Pallas kernels, gather_call(): pl.pallas_call(functools.partial(gather_kernel, n_chip), in_specs=[pl.Blo...  54 us
    ppermute x2, waiting for transfers between devices, local(): lax.ppermute(grads[i + 1], 'dp', swap).astype(jnp.float32)  40.7 us
    pallas_call x1, Pallas kernels, scatter_call(): pl.pallas_call(functools.partial(scatter_kernel, n_chip), in_specs=[whole...  34.4 us
    pallas_call x1, Pallas kernels, rows_call(): pl.pallas_call(functools.partial(rows_kernel, split), grid=(rows,), in_sp...  20.8 us
    add x2, other arithmetic, local(): grads[i].astype(jnp.float32)  5.22 us
  transfers between devices with their start and end apart: 2, of which 2 were waited for; matrix products, arithmetic and copies ran while one was open for 2% of the time, Pallas kernels for 21%

profile of v3, /device:TPU:0, one launch (start us, length us, event | category | flops | bytes accessed | tf_op | source)
XLA Modules:
  0.0 160.7 jit_solution(2092821053892776724)
XLA Ops:
  0.6 54.0 %shard_map.85 = (bf16[16,256,512]{2,1,0:T(8,128)(2,1)}, bf16[16,256,512]{2,1,0:T(8,128)(2,1)}) custom-call(bf16[256,512]{1,0:T(8,128)(2,1)} %x_ref.1, bf16[256,512]{1,0:T(8,128)(2,1)} %dy_ref.1), custom_call_target="tpu_custom_call" | custom-call | tf_op jit(solution)/shard_map/pallas_call | solution.py:229
  54.7 20.8 %shard_map.86 = (bf16[16,256,512]{2,1,0:T(8,128)(2,1)}, bf16[7,16,64,128]{3,2,1,0:T(8,128)(2,1)}, bf16[7,16,64,128]{3,2,1,0:T(8,128)(2,1)}, bf16[7,16,64,128]{3,2,1,0:T(8,128)(2,1)}, bf16[7,16,64,128]{3,2,1,0:T(8,128)(2,1)}) custom-call(s32[7,16]{1,0:T(8,128)} %up_cols.1, s32[7,16]{1,0:T(8,128)} %down_cols.1, s32[1]{0:T(128)} %bitcast.me, ...), custom_call_target="tpu_custom_call" | custom-call | flops 4697620480 | bytes 31457280 | tf_op jit(solution)/shard_map/pallas_call | solution.py:94
  75.5 1.5 collective-permute-start
  77.0 0.5 collective-permute-start.1
  77.5 0.0 copy-start
  77.5 2.2 %copy-done = bf16[16,256,512]{2,1,0:T(8,128)(2,1)S(1)} copy-done((bf16[16,256,512]{2,1,0:T(8,128)(2,1)S(1)}, bf16[16,256,512]{2,1,0:T(8,128)(2,1)}, u32[]{:S(2)}) %copy-start) | copy-done | bytes 4194328
  79.7 0.0 copy-start.2
  79.7 34.4 %shard_map.87 = bf16[256,512]{1,0:T(8,128)(2,1)S(1)} custom-call(bf16[16,256,512]{2,1,0:T(8,128)(2,1)S(1)} %copy-done), custom_call_target="tpu_custom_call" | custom-call | flops 2097152 | bytes 125829120 | tf_op jit(solution)/shard_map/pallas_call | solution.py:400
  114.1 4.5 %collective-permute-done = bf16[7,16,64,128]{3,2,1,0:T(8,128)(2,1)S(1)} collective-permute-done((bf16[7,16,64,128]{3,2,1,0:T(8,128)(2,1)}, bf16[7,16,64,128]{3,2,1,0:T(8,128)(2,1)S(1)}, u32[]{:S(2)}, u32[]{:S(2)}) %collective-permute-start) | collective-permute-done | bytes 1835040 | tf_op jit(solution)/shard_map/ppermute | solution.py:427
  118.6 0.0 copy-done.2
  118.6 0.0 copy-start.1
  118.6 2.6 %convert_add_fusion.1 = f32[7,16,64,128]{3,2,1,0:T(8,128)} fusion(bf16[7,16,64,128]{3,2,1,0:T(8,128)(2,1)S(1)} %collective-permute-done, bf16[7,16,64,128]{3,2,1,0:T(8,128)(2,1)S(1)} %copy-done.2), kind=kLoop, calls=%fused_computation.1 | loop fusion | flops 2752512 | bytes 7340032 | tf_op jit(solution)/shard_map/add | solution.py:426
  121.2 36.2 %collective-permute-done.1 = bf16[7,16,64,128]{3,2,1,0:T(8,128)(2,1)S(1)} collective-permute-done((bf16[7,16,64,128]{3,2,1,0:T(8,128)(2,1)}, bf16[7,16,64,128]{3,2,1,0:T(8,128)(2,1)S(1)}, u32[]{:S(2)}, u32[]{:S(2)}) %collective-permute-start.1) | collective-permute-done | bytes 1835040 | tf_op jit(solution)/shard_map/ppermute | solution.py:427
  157.4 0.0 copy-done.1
  157.4 2.6 %convert_add_fusion = f32[7,16,64,128]{3,2,1,0:T(8,128)} fusion(bf16[7,16,64,128]{3,2,1,0:T(8,128)(2,1)S(1)} %collective-permute-done.1, bf16[7,16,64,128]{3,2,1,0:T(8,128)(2,1)S(1)} %copy-done.1), kind=kLoop, calls=%fused_computation | loop fusion | flops 2752512 | bytes 7340032 | tf_op jit(solution)/shard_map/add | solution.py:426
  160.0 0.7 copy.10
Async XLA Ops:
  75.5 43.1 %collective-permute-start = (bf16[7,16,64,128]{3,2,1,0:T(8,128)(2,1)}, bf16[7,16,64,128]{3,2,1,0:T(8,128)(2,1)S(1)}, u32[]{:S(2)}, u32[]{:S(2)}) collective-permute-start(bf16[7,16,64,128]{3,2,1,0:T(8,128)(2,1)} %get-tuple-element.14), channel_id=1, source_target_pairs={{0,16},{16,0},{1,17},{17,1},{2,18},{18,2},{3,19},{19,3},{4,20},{20... | collective-permute-start | bytes 5505032 | tf_op jit(solution)/shard_map/ppermute | solution.py:427
  77.0 80.4 %collective-permute-start.1 = (bf16[7,16,64,128]{3,2,1,0:T(8,128)(2,1)}, bf16[7,16,64,128]{3,2,1,0:T(8,128)(2,1)S(1)}, u32[]{:S(2)}, u32[]{:S(2)}) collective-permute-start(bf16[7,16,64,128]{3,2,1,0:T(8,128)(2,1)} %get-tuple-element.16), channel_id=1, source_target_pairs={{0,16},{16,0},{1,17},{17,1},{2,18},{18,2},{3,19},{19,3},{4,20},{20... | collective-permute-start | bytes 5505032 | tf_op jit(solution)/shard_map/ppermute | solution.py:427
  77.5 2.2 %copy-start = (bf16[16,256,512]{2,1,0:T(8,128)(2,1)S(1)}, bf16[16,256,512]{2,1,0:T(8,128)(2,1)}, u32[]{:S(2)}) copy-start(bf16[16,256,512]{2,1,0:T(8,128)(2,1)} %get-tuple-element.12.part) | copy-start | bytes 12582916
  79.7 38.9 %copy-start.2 = (bf16[7,16,64,128]{3,2,1,0:T(8,128)(2,1)S(1)}, bf16[7,16,64,128]{3,2,1,0:T(8,128)(2,1)}, u32[]{:S(2)}) copy-start(bf16[7,16,64,128]{3,2,1,0:T(8,128)(2,1)} %get-tuple-element.13) | copy-start | bytes 5505028
  118.6 38.8 %copy-start.1 = (bf16[7,16,64,128]{3,2,1,0:T(8,128)(2,1)S(1)}, bf16[7,16,64,128]{3,2,1,0:T(8,128)(2,1)}, u32[]{:S(2)}) copy-start(bf16[7,16,64,128]{3,2,1,0:T(8,128)(2,1)} %get-tuple-element.15) | copy-start | bytes 5505028

commit v4 on v3

--- a/solution.py
+++ b/solution.py
@@ -417,21 +417,25 @@
 def local(n_dp, n_hst, n_chip, tokens, out_grad, up_blocks, up_cols, down_blocks, down_cols):
     whole_x, whole_dy = gather_call(n_hst, n_chip, tokens, out_grad)
     split = n_dp == 2
-    partial_value, *grads = rows_call(
-        split, whole_x, whole_dy, up_blocks, up_cols, down_blocks, down_cols
-    )
-    if split:
-        swap = [(0, 1), (1, 0)]
-        sums = [
-            grads[i].astype(jnp.float32)
-            + lax.ppermute(grads[i + 1], "dp", swap).astype(jnp.float32)
-            for i in (0, 2)
-        ]
-    else:
-        sums = [
-            lax.psum_scatter(g, "dp", scatter_dimension=2, tiled=True).astype(jnp.float32)
-            for g in grads
-        ]
+    rows = up_blocks.shape[0]
+    cuts = [slice(0, rows // 2), slice(rows // 2, rows)] if split else [slice(0, rows)]
+    parts, sums = [], [[], []]
+    for cut in cuts:
+        part, *grads = rows_call(
+            split, whole_x, whole_dy, up_blocks[cut], up_cols[cut], down_blocks[cut], down_cols[cut]
+        )
+        parts.append(part.astype(jnp.float32))
+        for i in range(2):
+            if split:
+                sent = lax.ppermute(grads[2 * i + 1], "dp", [(0, 1), (1, 0)])
+                both = grads[2 * i].astype(jnp.float32) + sent.astype(jnp.float32)
+            else:
+                both = lax.psum_scatter(
+                    grads[i], "dp", scatter_dimension=2, tiled=True
+                ).astype(jnp.float32)
+            sums[i].append(both)
+    sums = [jnp.concatenate(pieces, axis=0) for pieces in sums]
+    partial_value = sum(parts).astype(jnp.bfloat16)
     summed = scatter_call(n_hst, n_chip, partial_value)
     return (summed, *sums)
 

time: 161 us -> 161 us (level)
  waiting for transfers between devices: 40.7 us -> 15.1 us
  local copies, waits for them, and re-layouts: 2.9 us -> 15.1 us
  Pallas kernels: 109 us -> 116 us
  other arithmetic: 5.22 us -> 9.52 us
  starting transfers between devices: 2.06 us -> 4.13 us
    ppermute x2 -> x4, waiting for transfers between devices: 40.7 us -> 15.1 us  [local(): sent = lax.ppermute(grads[2 * i + 1], 'dp', [(0, 1), (1, 0)])]
    slice x0 -> x8, local copies, waits for them, and re-layouts: none -> 12.2 us  [the longest x2 4.29 us: local(): up_blocks[cut]]
    pallas_call x1 -> x2, Pallas kernels: 20.8 us -> 27.9 us  [rows_call(): pl.pallas_call(functools.partial(rows_kernel, split), grid=(rows,), in_sp...]
    concatenate x0 -> x2, other arithmetic: none -> 4.67 us  [local(): sums = [jnp.concatenate(pieces, axis=0) for pieces in sums]]
    add x2 -> x4, other arithmetic: 5.22 us -> 1.32 us  [local(): both = grads[2 * i].astype(jnp.float32) + sent.astype(jnp.float32)]
    convert_element_type x0 -> x1, other arithmetic: none -> 3.53 us  [local(): partial_value = sum(parts).astype(jnp.bfloat16)]
    ppermute x2 -> x4, starting transfers between devices: 2.06 us -> 4.13 us  [local(): sent = lax.ppermute(grads[2 * i + 1], 'dp', [(0, 1), (1, 0)])]
  transfers between devices with their start and end apart: 2 -> 4, of which waited for: 2 -> 1; matrix products, arithmetic and copies ran while one was open for 2% -> 7% of each run, Pallas kernels for 21% -> 31%
where the time goes in v4:
time: 161 us
  Pallas kernels  116 us (72%)
  local copies, waits for them, and re-layouts  15.1 us (9%)
  waiting for transfers between devices  15.1 us (9%)
  other arithmetic  9.52 us (6%)
  starting transfers between devices  4.13 us (3%)
    pallas_call x1, Pallas kernels, gather_call(): pl.pallas_call(functools.partial(gather_kernel, n_chip), in_specs=[pl.Blo...  54 us
    pallas_call x1, Pallas kernels, scatter_call(): pl.pallas_call(functools.partial(scatter_kernel, n_chip), in_specs=[whole...  34.5 us
    pallas_call x2, Pallas kernels, rows_call(): pl.pallas_call(functools.partial(rows_kernel, split), grid=(rows,), in_sp...  27.9 us
    ppermute x4, waiting for transfers between devices, local(): sent = lax.ppermute(grads[2 * i + 1], 'dp', [(0, 1), (1, 0)])  15.1 us
    concatenate x2, other arithmetic, local(): sums = [jnp.concatenate(pieces, axis=0) for pieces in sums]  4.67 us
    slice x2, local copies, waits for them, and re-layouts, local(): up_blocks[cut]  4.29 us
    slice x2, local copies, waits for them, and re-layouts, local(): down_blocks[cut]  4.18 us
    ppermute x4, starting transfers between devices, local(): sent = lax.ppermute(grads[2 * i + 1], 'dp', [(0, 1), (1, 0)])  4.13 us
  transfers between devices with their start and end apart: 4, of which 1 were waited for; matrix products, arithmetic and copies ran while one was open for 7% of the time, Pallas kernels for 31%

profile of v4, /device:TPU:0, one launch (start us, length us, event | category | flops | bytes accessed | tf_op | source)
XLA Modules:
  0.0 161.1 jit_solution(12202882430746559606)
XLA Ops:
  0.6 1.3 slice.24.up_cols
  1.9 1.3 slice.25.down_cols
  3.2 2.7 %slice.26.up_ref = bf16[3,16,128,128]{3,2,1,0:T(8,128)(2,1)} slice(bf16[7,16,128,128]{3,2,1,0:T(8,128)(2,1)} %param.8), slice={[0:3], [0:16], [0:128], [0:128]} | slice | bytes 3145728 | tf_op jit(solution)/shard_map/slice | solution.py:425
  5.9 2.7 %slice.27.down_ref = bf16[3,16,128,128]{3,2,1,0:T(8,128)(2,1)} slice(bf16[7,16,128,128]{3,2,1,0:T(8,128)(2,1)} %param.10), slice={[0:3], [0:16], [0:128], [0:128]} | slice | bytes 3145728 | tf_op jit(solution)/shard_map/slice | solution.py:425
  8.6 54.0 %shard_map.85 = (bf16[16,256,512]{2,1,0:T(8,128)(2,1)}, bf16[16,256,512]{2,1,0:T(8,128)(2,1)}) custom-call(bf16[256,512]{1,0:T(8,128)(2,1)} %x_ref.1, bf16[256,512]{1,0:T(8,128)(2,1)} %dy_ref.1), custom_call_target="tpu_custom_call" | custom-call | tf_op jit(solution)/shard_map/pallas_call | solution.py:229
  62.7 0.0 copy-start.7
  62.7 0.0 copy-start.8
  62.7 0.0 copy-start.1
  62.7 13.0 %shard_map.86 = (bf16[16,256,512]{2,1,0:T(8,128)(2,1)}, bf16[3,16,64,128]{3,2,1,0:T(8,128)(2,1)}, bf16[3,16,64,128]{3,2,1,0:T(8,128)(2,1)}, bf16[3,16,64,128]{3,2,1,0:T(8,128)(2,1)}, bf16[3,16,64,128]{3,2,1,0:T(8,128)(2,1)}) custom-call(s32[3,16]{1,0:T(4,128)} %slice.24.up_cols, s32[3,16]{1,0:T(4,128)} %slice.25.down_cols, s32[1]{0:T(128)} %bitcast.me, ...), custom_call_target="tpu_custom_call" | custom-call | flops 2013265920 | bytes 31457280 | tf_op jit(solution)/shard_map/pallas_call | solution.py:94
  75.7 1.5 collective-permute-start
  77.2 0.5 collective-permute-start.2
  77.8 0.0 copy-done.7
  77.8 0.6 slice.28.up_cols
  78.3 0.0 copy-done.8
  78.3 0.6 slice.29.down_cols
  78.9 0.0 copy-done.1
  78.9 0.0 copy-start.2
  78.9 1.6 slice.30.up_ref
  80.5 1.2 copy-done.2
  81.7 1.5 slice.31.down_ref
  83.2 0.0 copy-start
  83.2 14.9 %shard_map.87 = (bf16[16,256,512]{2,1,0:T(8,128)(2,1)}, bf16[4,16,64,128]{3,2,1,0:T(8,128)(2,1)}, bf16[4,16,64,128]{3,2,1,0:T(8,128)(2,1)}, bf16[4,16,64,128]{3,2,1,0:T(8,128)(2,1)}, bf16[4,16,64,128]{3,2,1,0:T(8,128)(2,1)}) custom-call(s32[4,16]{1,0:T(4,128)} %slice.28.up_cols, s32[4,16]{1,0:T(4,128)} %slice.29.down_cols, s32[1]{0:T(128)} %bitcast.me, ...), custom_call_target="tpu_custom_call" | custom-call | flops 2684354560 | bytes 31457280 | tf_op jit(solution)/shard_map/pallas_call | solution.py:94
  98.1 1.5 collective-permute-start.1
  99.7 0.5 collective-permute-start.3
  100.2 0.0 copy-done
  100.2 3.5 %add_convert_fusion.part = bf16[16,256,512]{2,1,0:T(8,128)(2,1)S(1)} fusion(bf16[16,256,512]{2,1,0:T(8,128)(2,1)} %get-tuple-element.18, bf16[16,256,512]{2,1,0:T(8,128)(2,1)S(1)} %copy-done), kind=kLoop, calls=%fused_computation | loop fusion | flops 8388608 | bytes 12582912 | tf_op jit(solution)/shard_map/convert_element_type | solution.py:438
  103.7 0.0 copy-start.6
  103.7 34.5 %shard_map.88 = bf16[256,512]{1,0:T(8,128)(2,1)S(1)} custom-call(bf16[16,256,512]{2,1,0:T(8,128)(2,1)S(1)} %add_convert_fusion.part), custom_call_target="tpu_custom_call" | custom-call | flops 2097152 | bytes 125829120 | tf_op jit(solution)/shard_map/pallas_call | solution.py:400
  138.2 0.0 copy-start.5
  138.2 0.0 collective-permute-done
  138.2 0.0 copy-done.6
  138.3 0.3 convert_add_fusion.3
  138.5 0.0 copy-start.4
  138.6 0.0 collective-permute-done.2
  138.6 0.8 copy-done.5
  139.4 0.3 convert_add_fusion.2
  139.6 0.0 collective-permute-done.1
  139.6 0.2 copy-done.4
  139.8 0.4 convert_add_fusion.1
  140.2 0.0 copy-start.3
  140.2 2.3 %pad_maximum_fusion = f32[7,16,64,128]{3,2,1,0:T(8,128)} fusion(f32[4,16,64,128]{3,2,1,0:T(8,128)S(1)} %convert_add_fusion.1, f32[3,16,64,128]{3,2,1,0:T(8,128)S(1)} %convert_add_fusion.3), kind=kLoop, calls=%fused_computation.1 | loop fusion | flops 917504 | bytes 7340032 | tf_op jit(solution)/shard_map/concatenate | solution.py:437
  142.6 15.1 %collective-permute-done.3 = bf16[4,16,64,128]{3,2,1,0:T(8,128)(2,1)S(1)} collective-permute-done((bf16[4,16,64,128]{3,2,1,0:T(8,128)(2,1)}, bf16[4,16,64,128]{3,2,1,0:T(8,128)(2,1)S(1)}, u32[]{:S(2)}, u32[]{:S(2)}) %collective-permute-start.3) | collective-permute-done | bytes 1048608 | tf_op jit(solution)/shard_map/ppermute | solution.py:430
  157.6 0.0 copy-done.3
  157.6 0.4 convert_add_fusion
  158.0 2.3 %pad_maximum_fusion.1 = f32[7,16,64,128]{3,2,1,0:T(8,128)} fusion(f32[4,16,64,128]{3,2,1,0:T(8,128)S(1)} %convert_add_fusion, f32[3,16,64,128]{3,2,1,0:T(8,128)S(1)} %convert_add_fusion.2), kind=kLoop, calls=%fused_computation.2 | loop fusion | flops 917504 | bytes 7340032 | tf_op jit(solution)/shard_map/concatenate | solution.py:437
  160.4 0.7 copy.10
Async XLA Ops:
  62.7 15.1 %copy-start.7 = (s32[7,16]{1,0:T(8,128)S(1)}, s32[7,16]{1,0:T(8,128)}, u32[]{:S(2)}) copy-start(s32[7,16]{1,0:T(8,128)} %param.9) | copy-start | bytes 1348
  62.7 15.7 %copy-start.8 = (s32[7,16]{1,0:T(8,128)S(1)}, s32[7,16]{1,0:T(8,128)}, u32[]{:S(2)}) copy-start(s32[7,16]{1,0:T(8,128)} %param.11) | copy-start | bytes 1348
  62.7 16.2 %copy-start.1 = (bf16[7,16,128,128]{3,2,1,0:T(8,128)(2,1)S(1)}, bf16[7,16,128,128]{3,2,1,0:T(8,128)(2,1)}, u32[]{:S(2)}) copy-start(bf16[7,16,128,128]{3,2,1,0:T(8,128)(2,1)} %param.8) | copy-start | bytes 11010052
  75.7 62.5 %collective-permute-start = (bf16[3,16,64,128]{3,2,1,0:T(8,128)(2,1)}, bf16[3,16,64,128]{3,2,1,0:T(8,128)(2,1)S(1)}, u32[]{:S(2)}, u32[]{:S(2)}) collective-permute-start(bf16[3,16,64,128]{3,2,1,0:T(8,128)(2,1)} %get-tuple-element.20), channel_id=1, source_target_pairs={{0,16},{16,0},{1,17},{17,1},{2,18},{18,2},{3,19},{19,3},{4,20},{20... | collective-permute-start | bytes 2359304 | tf_op jit(solution)/shard_map/ppermute | solution.py:430
  77.2 61.3 %collective-permute-start.2 = (bf16[3,16,64,128]{3,2,1,0:T(8,128)(2,1)}, bf16[3,16,64,128]{3,2,1,0:T(8,128)(2,1)S(1)}, u32[]{:S(2)}, u32[]{:S(2)}) collective-permute-start(bf16[3,16,64,128]{3,2,1,0:T(8,128)(2,1)} %get-tuple-element.24), channel_id=1, source_target_pairs={{0,16},{16,0},{1,17},{17,1},{2,18},{18,2},{3,19},{19,3},{4,20},{20... | collective-permute-start | bytes 2359304 | tf_op jit(solution)/shard_map/ppermute | solution.py:430
  78.9 2.8 %copy-start.2 = (bf16[7,16,128,128]{3,2,1,0:T(8,128)(2,1)S(1)}, bf16[7,16,128,128]{3,2,1,0:T(8,128)(2,1)}, u32[]{:S(2)}) copy-start(bf16[7,16,128,128]{3,2,1,0:T(8,128)(2,1)} %param.10) | copy-start | bytes 11010052
  83.2 17.0 %copy-start = (bf16[16,256,512]{2,1,0:T(8,128)(2,1)S(1)}, bf16[16,256,512]{2,1,0:T(8,128)(2,1)}, u32[]{:S(2)}) copy-start(bf16[16,256,512]{2,1,0:T(8,128)(2,1)} %get-tuple-element.17) | copy-start | bytes 12582916
  98.1 41.5 %collective-permute-start.1 = (bf16[4,16,64,128]{3,2,1,0:T(8,128)(2,1)}, bf16[4,16,64,128]{3,2,1,0:T(8,128)(2,1)S(1)}, u32[]{:S(2)}, u32[]{:S(2)}) collective-permute-start(bf16[4,16,64,128]{3,2,1,0:T(8,128)(2,1)} %get-tuple-element.22), channel_id=1, source_target_pairs={{0,16},{16,0},{1,17},{17,1},{2,18},{18,2},{3,19},{19,3},{4,20},{20... | collective-permute-start | bytes 3145736 | tf_op jit(solution)/shard_map/ppermute | solution.py:430
  99.7 58.0 %collective-permute-start.3 = (bf16[4,16,64,128]{3,2,1,0:T(8,128)(2,1)}, bf16[4,16,64,128]{3,2,1,0:T(8,128)(2,1)S(1)}, u32[]{:S(2)}, u32[]{:S(2)}) collective-permute-start(bf16[4,16,64,128]{3,2,1,0:T(8,128)(2,1)} %get-tuple-element.26), channel_id=1, source_target_pairs={{0,16},{16,0},{1,17},{17,1},{2,18},{18,2},{3,19},{19,3},{4,20},{20... | collective-permute-start | bytes 3145736 | tf_op jit(solution)/shard_map/ppermute | solution.py:430
  103.7 34.5 %copy-start.6 = (bf16[3,16,64,128]{3,2,1,0:T(8,128)(2,1)S(1)}, bf16[3,16,64,128]{3,2,1,0:T(8,128)(2,1)}, u32[]{:S(2)}) copy-start(bf16[3,16,64,128]{3,2,1,0:T(8,128)(2,1)} %get-tuple-element.19) | copy-start | bytes 2359300
  138.2 1.1 copy-start.5
  138.5 1.3 copy-start.4
  140.2 17.4 %copy-start.3 = (bf16[4,16,64,128]{3,2,1,0:T(8,128)(2,1)S(1)}, bf16[4,16,64,128]{3,2,1,0:T(8,128)(2,1)}, u32[]{:S(2)}) copy-start(bf16[4,16,64,128]{3,2,1,0:T(8,128)(2,1)} %get-tuple-element.25) | copy-start | bytes 3145732
